TPU v7x, 32 devices: a whole 2x2x4 slice. The times are simulated.
32 devices in a mesh: row: 8 (over z, core), col: 4 (over y, x).
Axes of the slice: x: 2, y: 2, z: 4, core: 2. Of those that a mesh axis runs over, the one named last changes fastest.
Arguments:
- shot_traces: float32 [16384, 2, 8192], P(('row', 'col')), may hold values from -0.046875 to 0.046875
- shot_ids: int32 [16384], P(('row', 'col')), may hold values from 0 to 8191, as said below
- shot_counts: int32 [32], P(('row', 'col')), may hold values from 0 to 512, as said below
- missing_blocks: int32 [64, 64], P('row', 'col'), may hold values from 0 to 1, as said below
- weight_bins: int32 [8192], P(('row', 'col')), may hold values from 0 to 63
- weight_table: float32 [64], replicated, may hold values from 0.1 to 1
- focus_panel: float32 [2, 8192, 512], P(None, ('col', 'row')), may hold values from -6 to 6
Outputs:
- wavefield: float32 [2, 8192, 512], P(None, ('row', 'col'))
- adjoint_image: float32 [2, 8192, 512], P(None, ('col', 'row'))
Inputs may be any that keep to these rules, and one draw needn't show every extreme that they name: `shot_ids`: over the counted slots of all devices every source appears exactly once; uncounted slots hold arbitrary sources. The counted slots of one device hold at most 64 sources of any block of 1024 consecutive sources, and at most (128) of any block of 2048; some device reaches both. `shot_counts`: some device has all 512 slots counted. `missing_blocks`: diagonal blocks are recorded, and of two mirrored blocks at most one is missing.
All inputs are finite; a program needn't handle non-finite values.
Results may differ from a plain program's by a relative error of at most 0.00007.
Values sent between devices are 32-bit elements; how exact they have to be, the bound alone decides.
A program may use at most 320 MiB of HBM per device.

v0:
```python
import jax
import jax.numpy as jnp
from jax import lax
from jax.sharding import PartitionSpec as P


def high_dot(left, right):
    return jnp.dot(left, right, precision=lax.Precision.HIGHEST, preferred_element_type=jnp.float32)


def trans_dot(left, right):
    return lax.dot_general(
        left,
        right,
        (((0,), (0,)), ((), ())),
        precision=lax.Precision.HIGHEST,
        preferred_element_type=jnp.float32,
    )


def pack_slots(traces, labels, held_count, group_size, group_count, capacity):
    slot_total = labels.shape[0]
    slot_index = jnp.arange(slot_total, dtype=jnp.int32)
    is_used = slot_index < held_count
    dest_group = labels // group_size
    onehot = (
        (dest_group[:, None] == jnp.arange(group_count, dtype=jnp.int32)[None, :])
        & is_used[:, None]
    ).astype(jnp.int32)
    before = jnp.cumsum(onehot, axis=0) - onehot
    rank_in = jnp.sum(before * onehot, axis=1)
    position = jnp.where(is_used, dest_group * capacity + rank_in, group_count * capacity)
    source = (
        jnp.full((group_count * capacity,), slot_total, jnp.int32)
        .at[position]
        .set(slot_index, mode="drop")
    )
    packed = jnp.take(traces, source, axis=0, mode="fill", fill_value=0.0)
    packed_labels = jnp.take(labels, source, axis=0, mode="fill", fill_value=-1)
    return (packed, packed_labels)


def place_rows(arrived, labels, first_label, length):
    has_label = labels >= 0
    target = jnp.where(has_label, labels - first_label, length)
    source = (
        jnp.zeros((length,), jnp.int32)
        .at[target]
        .set(jnp.arange(labels.shape[0], dtype=jnp.int32), mode="drop")
    )
    return jnp.take(arrived, source, axis=0)


def lookup(bins, table):
    matches = bins[:, None] == jnp.arange(table.shape[0], dtype=jnp.int32)[None, :]
    return jnp.sum(jnp.where(matches, table[None, :], 0.0), axis=1)


def local(
    shot_traces, shot_ids, shot_counts, missing_blocks, weight_bins, weight_table, focus_panel
):
    slot_total = shot_traces.shape[0]
    stations = shot_traces.shape[2]
    row_count = lax.axis_size("row")
    col_count = lax.axis_size("col")
    src_tile = stations // row_count
    rcv_tile = stations // col_count
    row_index = lax.axis_index("row")
    col_index = lax.axis_index("col")
    held_count = shot_counts[0]
    packed, packed_labels = pack_slots(
        shot_traces, shot_ids, held_count, src_tile, row_count, slot_total // row_count
    )
    outgoing = packed.reshape(slot_total, 2, col_count, rcv_tile)
    label_copies = jnp.broadcast_to(packed_labels[:, None, None], (slot_total, 1, col_count))
    arrived, arrived_labels = (
        lax.all_to_all(
            lax.all_to_all(outgoing, "row", split_axis=0, concat_axis=0, tiled=True),
            "col",
            split_axis=2,
            concat_axis=0,
            tiled=True,
        ),
        lax.all_to_all(
            lax.all_to_all(label_copies, "row", split_axis=0, concat_axis=0, tiled=True),
            "col",
            split_axis=2,
            concat_axis=0,
            tiled=True,
        ),
    )
    direct = place_rows(
        arrived.reshape(-1, 2, rcv_tile), arrived_labels.reshape(-1), row_index * src_tile, src_tile
    )
    capacity_rec = slot_total // col_count
    packed_mirror, mirror_labels = pack_slots(
        shot_traces, shot_ids, held_count, rcv_tile, col_count, capacity_rec
    )
    mirror_out = packed_mirror.reshape(slot_total, 2, row_count, src_tile)
    mirror_copies = jnp.broadcast_to(mirror_labels[:, None, None], (slot_total, 1, row_count))
    halfway, halfway_labels = (
        lax.all_to_all(mirror_out, "row", split_axis=2, concat_axis=0, tiled=True),
        lax.all_to_all(mirror_copies, "row", split_axis=2, concat_axis=0, tiled=True),
    )
    halfway = halfway.reshape(row_count, col_count, capacity_rec, 2, src_tile)
    halfway_labels = halfway_labels.reshape(row_count, col_count, capacity_rec)
    mirrored, mirrored_labels = (
        lax.all_to_all(halfway, "col", split_axis=1, concat_axis=0, tiled=True),
        lax.all_to_all(halfway_labels, "col", split_axis=1, concat_axis=0, tiled=True),
    )
    transposed = place_rows(
        mirrored.reshape(-1, 2, src_tile),
        mirrored_labels.reshape(-1),
        col_index * rcv_tile,
        rcv_tile,
    )
    blocks_down = missing_blocks.shape[0]
    blocks_across = missing_blocks.shape[1]
    block_size = src_tile // blocks_down
    is_missing = jnp.broadcast_to(
        missing_blocks[:, None, :, None] > 0, (blocks_down, block_size, blocks_across, block_size)
    ).reshape(src_tile, rcv_tile)
    kernel_re = jnp.where(is_missing, transposed[:, 0, :].T, direct[:, 0, :])
    kernel_im = jnp.where(is_missing, transposed[:, 1, :].T, direct[:, 1, :])
    focus_all = lax.all_gather(focus_panel, "row", axis=1, tiled=True)
    panel_re = focus_all[0]
    panel_im = focus_all[1]
    field_re = high_dot(kernel_re, panel_re) - high_dot(kernel_im, panel_im)
    field_im = high_dot(kernel_re, panel_im) + high_dot(kernel_im, panel_re)
    own_rows = lax.psum_scatter(
        jnp.stack([field_re, field_im], axis=1), "col", scatter_dimension=0, tiled=True
    )
    weighted = own_rows * lookup(weight_bins, weight_table)[:, None, None]
    weighted_all = lax.all_gather(weighted, "col", axis=0, tiled=True)
    weighted_re = weighted_all[:, 0, :]
    weighted_im = weighted_all[:, 1, :]
    image_re = trans_dot(kernel_re, weighted_re) + trans_dot(kernel_im, weighted_im)
    image_im = trans_dot(kernel_re, weighted_im) - trans_dot(kernel_im, weighted_re)
    image_rows = lax.psum_scatter(
        jnp.stack([image_re, image_im], axis=1), "row", scatter_dimension=0, tiled=True
    )
    return (jnp.swapaxes(own_rows, 0, 1), jnp.swapaxes(image_rows, 0, 1))


def solution(mesh):
    placed = (
        P(("row", "col"), None, None),
        P(("row", "col")),
        P(("row", "col")),
        P("row", "col"),
        P(("row", "col")),
        P(),
        P(None, ("col", "row"), None),
    )
    return jax.shard_map(
        local,
        mesh=mesh,
        in_specs=placed,
        out_specs=(P(None, ("row", "col"), None), P(None, ("col", "row"), None)),
        check_vma=False,
    )
```

profile of v0, /device:TPU:0, one launch (start us, length us, event | category | flops | bytes accessed | tf_op | source)
XLA Modules:
  0.0 3004.8 jit_solution(7320027503806781261)
XLA Ops:
  7.2 0.7 add_select_fusion.1
  8.5 1.2 reduce-window.14
  10.3 1.1 reduce-window.16
  11.8 2.4 scatter_custom_fusion.2
  14.3 3.6 gather_fusion.4
  17.9 1.6 broadcast_in_dim.115
  20.0 1.3 reduce.4
  21.3 0.8 reshape.312
  22.1 6.4 all-to-all-start.4
  28.4 2.4 scatter_custom_fusion
  30.9 3.6 gather_fusion.2
  35.1 5.1 all-to-all-start
  41.4 0.7 copy.63
  42.1 3.8 all-to-all-done
  45.9 3.7 all-to-all-start.5
  49.6 45.2 %gather_fusion.3 = f32[512,2,8192]{2,1,0:T(2,128)} fusion(f32[512,2,8192]{2,1,0:T(2,128)} %param.11, s32[1024]{0:T(1024)S(1)} %pad_clamp_fusion.1), kind=kCustom, calls=%fused_computation.1.clone | custom fusion | bytes 67110912 | tf_op jit(solution)/shard_map/jit(_take)/gather | solution.py:38
  96.1 4.1 all-to-all-start.1
  100.2 24.2 broadcast_select_fusion.1
  124.4 48.8 %copy.56 = f32[512,2,8192]{0,2,1:T(8,128)} copy(f32[512,2,8192]{2,1,0:T(2,128)} %broadcast_select_fusion.1) | data formatting | bytes 67108864 | tf_op jit(solution)/shard_map/jit(_take)/select_n | solution.py:38
  173.1 22.9 copy.57
  196.6 7.3 all-to-all-start.2
  203.9 46.5 %gather_fusion.5 = f32[512,2,8192]{2,1,0:T(2,128)} fusion(f32[512,2,8192]{2,1,0:T(2,128)} %param.11, s32[1024]{0:T(1024)S(1)} %pad_clamp_fusion), kind=kCustom, calls=%fused_computation.3.clone | custom fusion | bytes 67110912 | tf_op jit(solution)/shard_map/jit(_take)/gather | solution.py:38
  250.5 24.2 broadcast_select_fusion
  274.6 48.7 %copy.64 = f32[512,2,8192]{0,2,1:T(8,128)} copy(f32[512,2,8192]{2,1,0:T(2,128)} %broadcast_select_fusion) | data formatting | bytes 67108864 | tf_op jit(solution)/shard_map/jit(_take)/select_n | solution.py:38
  323.4 39.8 %copy.65 = f32[512,2,4,2048]{3,2,1,0:T(4,128)} copy(f32[512,2,4,2048]{0,3,2,1:T(8,128)} %bitcast.133) | data formatting | bytes 67108864 | tf_op jit(solution)/shard_map/reshape | solution.py:74
  363.2 563.9 %all-to-all-done.2 = f32[512,2,8,1024]{0,3,1,2:T(8,128)} async-done(((f32[512,2,8,1024]{0,3,1,2:T(8,128)}), f32[512,2,8,1024]{0,3,1,2:T(8,128)}, u32[]{:S(2)}, u32[]{:S(2)}) %all-to-all-start.2) | async-done | bytes 33554464 | tf_op jit(solution)/shard_map/all_to_all | solution.py:102
  927.1 7.1 all-to-all-start.6
  934.2 31.9 %copy.58 = f32[512,2,8,1024]{3,0,1,2:T(8,128)} copy(f32[512,2,8,1024]{0,3,1,2:T(8,128)} %all-to-all-done.2) | data formatting | bytes 67108864 | tf_op jit(solution)/shard_map/all_to_all | solution.py:102
  966.1 23.4 copy.59
  989.5 667.9 %all-to-all-done.6 = f32[512,2,4,2048]{3,2,1,0:T(4,128)} async-done(((f32[512,2,4,2048]{3,2,1,0:T(4,128)}), f32[512,2,4,2048]{3,2,1,0:T(4,128)}, u32[]{:S(2)}, u32[]{:S(2)}) %all-to-all-start.6) | async-done | bytes 33554464 | tf_op jit(solution)/shard_map/all_to_all | solution.py:78
  1657.4 9.7 all-to-all-start.3
  1667.1 37.9 %copy.66 = f32[512,2,4,2048]{0,3,1,2:T(8,128)} copy(f32[512,2,4,2048]{3,2,1,0:T(4,128)} %all-to-all-done.6) | data formatting | bytes 67108864 | tf_op jit(solution)/shard_map/all_to_all | solution.py:78
  1705.0 324.4 %all-to-all-done.3 = f32[8,4,128,2,1024]{4,2,3,0,1:T(8,128)} async-done(((f32[8,4,128,2,1024]{4,2,3,0,1:T(8,128)}), f32[8,4,128,2,1024]{4,2,3,0,1:T(8,128)}, u32[]{:S(2)}, u32[]{:S(2)}) %all-to-all-start.3) | async-done | bytes 33554464 | tf_op jit(solution)/shard_map/all_to_all | solution.py:108
  2029.4 9.7 all-to-all-start.7
  2039.1 0.7 all-gather.3.cloned.1.call-update
  2040.0 8.0 scatter_custom_fusion.3
  2048.2 15.9 scatter_custom_fusion.1
  2064.1 23.5 copy.60
  2087.6 55.0 %copy.61 = f32[4096,2,1024]{2,1,0:T(2,128)} copy(f32[4096,2,1024]{2,0,1:T(8,128)} %bitcast.135) | data formatting | bytes 67108864 | tf_op jit(solution)/shard_map/reshape | solution.py:112
  2142.7 258.0 %all-to-all-done.7 = f32[512,2,4,2048]{0,3,1,2:T(8,128)} async-done(((f32[512,2,4,2048]{0,3,1,2:T(8,128)}), f32[512,2,4,2048]{0,3,1,2:T(8,128)}, u32[]{:S(2)}, u32[]{:S(2)}) %all-to-all-start.7) | async-done | bytes 33554464 | tf_op jit(solution)/shard_map/all_to_all | solution.py:77
  2400.6 31.8 %copy.67 = f32[512,2,4,2048]{3,0,2,1:T(8,128)} copy(f32[512,2,4,2048]{0,3,1,2:T(8,128)} %all-to-all-done.7) | data formatting | bytes 67108864 | tf_op jit(solution)/shard_map/all_to_all | solution.py:77
  2432.4 55.0 %copy.68 = f32[2048,2,2048]{2,1,0:T(2,128)} copy(f32[2048,2,2048]{2,0,1:T(8,128)} %bitcast.136) | data formatting | bytes 67108864 | tf_op jit(solution)/shard_map/reshape | solution.py:93
  2487.5 39.4 %gather_fusion.1 = f32[1024,2,2048]{2,1,0:T(2,128)} fusion(f32[2048,2,2048]{2,1,0:T(2,128)} %copy.68, s32[1024]{0:T(1024)S(1)} %fusion.22), kind=kCustom, calls=%fused_computation.5 | custom fusion | bytes 33558528 | tf_op jit(solution)/shard_map/jit(_take)/gather | solution.py:51
  2526.9 25.0 copy.69
  2551.9 54.2 %gather_fusion = f32[2048,2,1024]{2,1,0:T(2,128)} fusion(f32[4096,2,1024]{2,1,0:T(2,128)} %copy.61, s32[2048]{0:T(1024)S(1)} %fusion.19), kind=kCustom, calls=%fused_computation.4 | custom fusion | bytes 33562624 | tf_op jit(solution)/shard_map/jit(_take)/gather | solution.py:51
  2606.1 12.4 broadcast_select_fusion.3
  2618.5 4.1 copy-done.1
  2622.6 13.1 broadcast_select_fusion.2
  2635.7 19.2 fusion.31
  2655.6 17.8 fusion.1
  2673.4 16.7 fusion.3
  2690.2 13.8 fusion.2
  2704.0 13.6 subtract_bitcast_fusion.1
  2717.6 13.8 add_bitcast_fusion.1
  2731.3 2.4 pad_maximum_fusion.1
  2733.9 51.4 %reduce-scatter.3.cloned.1.call-done = f32[256,2,512]{2,0,1:T(8,128)} async-done(((f32[1024,2,512]{2,0,1:T(8,128)}), f32[256,2,512]{2,0,1:T(8,128)}) %reduce-scatter.3.cloned.1.call-update) | async-done | bytes 1048592 | tf_op jit(solution)/shard_map/reduce_scatter | solution.py:130
  2785.3 2.3 broadcast_multiply_fusion
  2787.7 52.7 %all-gather.5.cloned.1.call-done = f32[1024,2,512]{2,0,1:T(8,128)} async-done(((f32[256,2,512]{2,0,1:T(8,128)}), f32[1024,2,512]{2,0,1:T(8,128)}) %all-gather.5.cloned.1.call-update) | async-done | bytes 4194320 | tf_op jit(solution)/shard_map/all_gather | solution.py:134
  2840.4 17.2 fusion.6
  2857.7 16.0 fusion.7
  2873.7 15.1 add_bitcast_fusion
  2888.8 15.1 subtract_bitcast_fusion
  2904.0 4.2 pad_maximum_fusion
  2908.2 89.7 %reduce-scatter.5.cloned.1.call-done = f32[256,2,512]{2,0,1:T(8,128)} async-done(((f32[2048,2,512]{2,0,1:T(8,128)}), f32[256,2,512]{2,0,1:T(8,128)}) %reduce-scatter.5.cloned.1.call-update) | async-done | bytes 1048592 | tf_op jit(solution)/shard_map/reduce_scatter | solution.py:139
  (82 shorter events, 6.1 us)
Async XLA Ops:
  22.1 12.5 all-to-all-start.4
  35.1 10.7 all-to-all-start
  45.9 49.6 %all-to-all-start.5 = ((s32[512,1,4]{0,1,2:T(1,128)}), s32[512,1,4]{0,1,2:T(1,128)S(1)}, u32[]{:S(2)}, u32[]{:S(2)}) async-start(s32[512,1,4]{0,1,2:T(1,128)} %copy.63), calls=%async_computation.5 | async-start | bytes 16384 | tf_op jit(solution)/shard_map/all_to_all | solution.py:84
  95.5 0.6 copy-start.5
  96.1 100.0 %all-to-all-start.1 = ((s32[8,4,128]{2,0,1:T(8,128)}), s32[8,4,128]{2,0,1:T(8,128)S(1)}, u32[]{:S(2)}, u32[]{:S(2)}) async-start(s32[8,4,128]{2,0,1:T(8,128)} %bitcast.127), calls=%async_computation.1 | async-start | bytes 32768 | tf_op jit(solution)/shard_map/all_to_all | solution.py:109
  196.0 0.6 copy-start.3
  196.6 730.5 %all-to-all-start.2 = ((f32[512,2,8,1024]{0,3,1,2:T(8,128)}), f32[512,2,8,1024]{0,3,1,2:T(8,128)}, u32[]{:S(2)}, u32[]{:S(2)}) async-start(f32[512,2,8,1024]{0,3,1,2:T(8,128)} %copy.57), calls=%async_computation.2 | async-start | bytes 67108864 | tf_op jit(solution)/shard_map/all_to_all | solution.py:102
  927.1 730.3 %all-to-all-start.6 = ((f32[512,2,4,2048]{3,2,1,0:T(4,128)}), f32[512,2,4,2048]{3,2,1,0:T(4,128)}, u32[]{:S(2)}, u32[]{:S(2)}) async-start(f32[512,2,4,2048]{3,2,1,0:T(4,128)} %copy.65), calls=%async_computation.6 | async-start | bytes 67108864 | tf_op jit(solution)/shard_map/all_to_all | solution.py:78
  1657.4 372.0 %all-to-all-start.3 = ((f32[8,4,128,2,1024]{4,2,3,0,1:T(8,128)}), f32[8,4,128,2,1024]{4,2,3,0,1:T(8,128)}, u32[]{:S(2)}, u32[]{:S(2)}) async-start(f32[8,4,128,2,1024]{4,2,3,0,1:T(8,128)} %copy.59), calls=%async_computation.3 | async-start | bytes 67108864 | tf_op jit(solution)/shard_map/all_to_all | solution.py:108
  1705.0 334.9 %copy-start.7 = (s32[8,16]{1,0:T(8,128)S(1)}, s32[8,16]{1,0:T(8,128)}, u32[]{:S(2)}) copy-start(s32[8,16]{1,0:T(8,128)} %param.14) | copy-start | bytes 1540
  1705.0 335.0 %copy-start.6 = (s32[512,1,4]{0,1,2:T(1,128)S(1)}, s32[512,1,4]{0,1,2:T(1,128)}, u32[]{:S(2)}) copy-start(s32[512,1,4]{0,1,2:T(1,128)} %copy-done.5) | copy-start | bytes 24580
  1705.0 343.1 %copy-start.4 = (s32[8,4,128]{2,0,1:T(8,128)S(1)}, s32[8,4,128]{2,0,1:T(8,128)}, u32[]{:S(2)}) copy-start(s32[8,4,128]{2,0,1:T(8,128)} %copy-done.3) | copy-start | bytes 49156
  2029.4 371.3 %all-to-all-start.7 = ((f32[512,2,4,2048]{0,3,1,2:T(8,128)}), f32[512,2,4,2048]{0,3,1,2:T(8,128)}, u32[]{:S(2)}, u32[]{:S(2)}) async-start(f32[512,2,4,2048]{0,3,1,2:T(8,128)} %copy.66), calls=%async_computation.7 | async-start | bytes 67108864 | tf_op jit(solution)/shard_map/all_to_all | solution.py:77
  2039.1 634.3 %all-gather.3.cloned.1.call-start = ((), (), s32[]{:S(2)}) async-start(), calls=%async_computation.10 | async-start | bytes 9437184 | tf_op jit(solution)/shard_map/all_gather | solution.py:125
  2039.8 745.5 %reduce-scatter.3.cloned.1.call-start = ((), (), s32[]{:S(2)}) async-start(), calls=%async_computation.11 | async-start | bytes 5242880 | tf_op jit(solution)/shard_map/reduce_scatter | solution.py:130
  2606.1 16.5 copy-start.1
  2673.4 16.8 copy-start
  2673.4 16.8 copy-start.10
  2690.2 27.4 slice-start.2
  2703.9 13.6 slice-start.3
  2731.3 2.5 copy-start.8
  2731.3 2.5 copy-start.9
  2733.8 106.6 %all-gather.5.cloned.1.call-start = ((), (), s32[]{:S(2)}) async-start(), calls=%async_computation.12 | async-start | bytes 5242880 | tf_op jit(solution)/shard_map/all_gather | solution.py:134
  2787.7 210.2 %reduce-scatter.5.cloned.1.call-start = ((), (), s32[]{:S(2)}) async-start(), calls=%async_computation.13 | async-start | bytes 9437184 | tf_op jit(solution)/shard_map/reduce_scatter | solution.py:139
  2840.4 17.3 copy-start.2
  2840.4 33.3 %slice-start = ((s8[8388608]{0:T(1024)(128)(4,1)}), s8[4194304]{0:T(1024)(128)(4,1)S(1)}, s32[]{:S(2)}) async-start(s8[8388608]{0:T(1024)(128)(4,1)} %bitcast.137), calls=%async_computation.14 | async-start | bytes 8388608
  2857.7 16.0 slice-start.1
Sparse Core Ops, SparseCore 0:
  2041.5 81.8 all-gather.2
  2733.9 51.3 reduce-scatter.2
  2787.8 52.5 all-gather.4
  2908.3 89.5 reduce-scatter.4
where the time goes:
time: 3020 us; the launch traced here: 3000 us
  waiting for transfers between devices  2010 us (67%)
  local copies, waits for them, and re-layouts  696 us (23%)
  matrix products  121 us (4%)
  other arithmetic  106 us (4%)
  starting transfers between devices  53.3 us (2%)
    all_to_all x1, waiting for transfers between devices, local(): lax.all_to_all(outgoing, 'row', split_axis=0, concat_axis=0, tiled=True)  668 us
    all_to_all x1, waiting for transfers between devices, local(): lax.all_to_all(mirror_out, 'row', split_axis=2, concat_axis=0, tiled=True)  564 us
    all_to_all x1, waiting for transfers between devices, local(): lax.all_to_all(halfway, 'col', split_axis=1, concat_axis=0, tiled=True)  324 us
    all_to_all x1, waiting for transfers between devices, local(): lax.all_to_all(lax.all_to_all(outgoing, 'row', split_axis=0, concat_axis=...  258 us
    gather x3, local copies, waits for them, and re-layouts, place_rows(): return jnp.take(arrived, source, axis=0)  119 us
    select_n x2, local copies, waits for them, and re-layouts, pack_slots(): packed = jnp.take(traces, source, axis=0, mode='fill', fill_value=0.0)  97.5 us
    gather x2, local copies, waits for them, and re-layouts, pack_slots(): packed = jnp.take(traces, source, axis=0, mode='fill', fill_value=0.0)  91.8 us
    reduce_scatter x1, waiting for transfers between devices, local(): lax.psum_scatter(jnp.stack([image_re, image_im], axis=1), 'row', scatter_...  89.7 us
  transfers between devices with their start and end apart: 12, of which 8 were waited for; matrix products, arithmetic and copies ran while one was open for 26% of the time, Pallas kernels for 0%

commit v1 on v0

--- a/solution.py
+++ b/solution.py
@@ -2,6 +2,29 @@
 import jax.numpy as jnp
 from jax import lax
 from jax.sharding import PartitionSpec as P
+
+
+def cut_along(array, dim, devices):
+    shape = array.shape
+    blocks = array.reshape(*shape[:dim], devices, shape[dim] // devices, *shape[dim + 1 :])
+    return jnp.moveaxis(blocks, dim, 0)
+
+
+def joined_along(parts, dim):
+    lengths = list(parts.shape[1:])
+    lengths[dim] *= parts.shape[0]
+    return jnp.moveaxis(parts, 0, dim).reshape(lengths)
+
+
+def swapped_with_each(x, axis, split_dim, concat_dim):
+    size, index = (lax.axis_size(axis), lax.axis_index(axis))
+    pieces = cut_along(x, split_dim, size)
+    outs = [pieces[index]]
+    for step in range(1, size):
+        sent = pieces[index ^ step]
+        outs.append(lax.ppermute(sent, axis, [(i, i ^ step) for i in range(size)]))
+    pieces = jnp.stack(outs)[index ^ jnp.arange(size)]
+    return joined_along(pieces, concat_dim)
 
 
 def high_dot(left, right):
@@ -74,12 +97,8 @@
     outgoing = packed.reshape(slot_total, 2, col_count, rcv_tile)
     label_copies = jnp.broadcast_to(packed_labels[:, None, None], (slot_total, 1, col_count))
     arrived, arrived_labels = (
-        lax.all_to_all(
-            lax.all_to_all(outgoing, "row", split_axis=0, concat_axis=0, tiled=True),
-            "col",
-            split_axis=2,
-            concat_axis=0,
-            tiled=True,
+        swapped_with_each(
+            lax.all_to_all(outgoing, "row", split_axis=0, concat_axis=0, tiled=True), "col", 2, 0
         ),
         lax.all_to_all(
             lax.all_to_all(label_copies, "row", split_axis=0, concat_axis=0, tiled=True),

time: 3020 us -> 2660 us (0.88)
  waiting for transfers between devices: 2010 us -> 1580 us
  other arithmetic: 106 us -> 179 us
    all_to_all x1 -> x0, waiting for transfers between devices: 258 us -> none  [local(): lax.all_to_all(lax.all_to_all(outgoing, 'row', split_axis=0, concat_axis=...]
    all_to_all x1, waiting for transfers between devices: 324 us -> 96.5 us  [local(): lax.all_to_all(halfway, 'col', split_axis=1, concat_axis=0, tiled=True)]
    all_to_all x1, waiting for transfers between devices: 564 us -> 702 us  [local(): lax.all_to_all(mirror_out, 'row', split_axis=2, concat_axis=0, tiled=True)]
    all_to_all x1, waiting for transfers between devices: 668 us -> 582 us  [local(): lax.all_to_all(outgoing, 'row', split_axis=0, concat_axis=0, tiled=True)]
    gather x0 -> x4, local copies, waits for them, and re-layouts: none -> 84.2 us  [swapped_with_each(): pieces = jnp.stack(outs)[index ^ jnp.arange(size)]]
    all_to_all x2 -> x0, local copies, waits for them, and re-layouts: 69.7 us -> none  [the longest x1 37.9 us: local(): lax.all_to_all(outgoing, 'row', split_axis=0, concat_axis=0, tiled=True)]
    dynamic_slice x0 -> x1, local copies, waits for them, and re-layouts: none -> 57.8 us  [swapped_with_each(): outs = [pieces[index]]]
    reshape x1 -> x0, local copies, waits for them, and re-layouts: 55 us -> none  [local(): arrived.reshape(-1, 2, rcv_tile)]
  transfers between devices with their start and end apart: 12 -> 14, of which waited for: 8 -> 7; matrix products, arithmetic and copies ran while one was open for 26% -> 32% of each run, Pallas kernels for 0% -> 0%
where the time goes in v1:
time: 2660 us; the launch traced here: 2640 us
  waiting for transfers between devices  1580 us (59%)
  local copies, waits for them, and re-layouts  701 us (26%)
  other arithmetic  179 us (7%)
  matrix products  121 us (5%)
  starting transfers between devices  46.6 us (2%)
    all_to_all x1, waiting for transfers between devices, local(): lax.all_to_all(mirror_out, 'row', split_axis=2, concat_axis=0, tiled=True)  702 us
    all_to_all x1, waiting for transfers between devices, local(): lax.all_to_all(outgoing, 'row', split_axis=0, concat_axis=0, tiled=True)  582 us
    gather x3, local copies, waits for them, and re-layouts, place_rows(): return jnp.take(arrived, source, axis=0)  119 us
    all_to_all x1, waiting for transfers between devices, local(): lax.all_to_all(halfway, 'col', split_axis=1, concat_axis=0, tiled=True)  96.5 us
    gather x2, local copies, waits for them, and re-layouts, pack_slots(): packed = jnp.take(traces, source, axis=0, mode='fill', fill_value=0.0)  91.7 us
    reduce_scatter x1, waiting for transfers between devices, local(): lax.psum_scatter(jnp.stack([image_re, image_im], axis=1), 'row', scatter_...  89.7 us
    gather x4, local copies, waits for them, and re-layouts, swapped_with_each(): pieces = jnp.stack(outs)[index ^ jnp.arange(size)]  84.2 us
    dot_general x4, matrix products, trans_dot(): lax.dot_general(left, right, (((0,), (0,)), ((), ())), precision=lax.Prec...  62.8 us
  transfers between devices with their start and end apart: 14, of which 7 were waited for; matrix products, arithmetic and copies ran while one was open for 32% of the time, Pallas kernels for 0%

profile of v1, /device:TPU:0, one launch (start us, length us, event | category | flops | bytes accessed | tf_op | source)
XLA Modules:
  0.0 2641.0 jit_solution(8462635906243502484)
XLA Ops:
  10.0 1.2 reduce-window.14
  11.8 2.4 scatter_custom_fusion.2
  14.3 3.6 gather_fusion.7
  17.9 1.6 broadcast_in_dim.116
  20.0 1.3 reduce.4
  22.1 6.4 all-to-all-start.4
  28.4 2.4 scatter_custom_fusion
  30.9 3.6 gather_fusion.5
  35.2 5.1 all-to-all-start
  42.1 3.8 all-to-all-done
  45.9 3.7 all-to-all-start.5
  49.6 46.5 %gather_fusion.8 = f32[512,2,8192]{2,1,0:T(2,128)} fusion(f32[512,2,8192]{2,1,0:T(2,128)} %param.11, s32[1024]{0:T(1024)S(1)} %pad_clamp_fusion.1), kind=kCustom, calls=%fused_computation.3.clone | custom fusion | bytes 67110912 | tf_op jit(solution)/shard_map/jit(_take)/gather | solution.py:61
  97.3 3.3 all-to-all-start.1
  100.6 24.2 broadcast_select_fusion
  124.8 45.8 %reshape.232 = f32[512,2,4,2048]{3,2,1,0:T(4,128)} reshape(f32[512,2,8192]{2,1,0:T(2,128)} %broadcast_select_fusion) | data formatting | bytes 67108864 | tf_op jit(solution)/shard_map/reshape | solution.py:97
  170.6 7.3 all-to-all-start.6
  177.9 45.2 %gather_fusion.6 = f32[512,2,8192]{2,1,0:T(2,128)} fusion(f32[512,2,8192]{2,1,0:T(2,128)} %param.11, s32[1024]{0:T(1024)S(1)} %pad_clamp_fusion.2), kind=kCustom, calls=%fused_computation.1.clone | custom fusion | bytes 67110912 | tf_op jit(solution)/shard_map/jit(_take)/gather | solution.py:61
  223.2 24.2 broadcast_select_fusion.1
  247.4 48.7 %copy.42 = f32[512,2,8192]{0,2,1:T(8,128)} copy(f32[512,2,8192]{2,1,0:T(2,128)} %broadcast_select_fusion.1) | data formatting | bytes 67108864 | tf_op jit(solution)/shard_map/jit(_take)/select_n | solution.py:61
  296.1 22.9 copy.43
  318.9 582.2 %all-to-all-done.6 = f32[512,2,4,2048]{3,2,1,0:T(4,128)} async-done(((f32[512,2,4,2048]{3,2,1,0:T(4,128)}), f32[512,2,4,2048]{3,2,1,0:T(4,128)}, u32[]{:S(2)}, u32[]{:S(2)}) %all-to-all-start.6) | async-done | bytes 33554464 | tf_op jit(solution)/shard_map/all_to_all | solution.py:101
  901.1 7.2 all-to-all-start.2
  908.4 57.8 %dynamic-slice_bitcast_fusion = (f32[1,512,2,1,2048]{4,3,2,1,0:T(1,128)}, f32[512,2,1,2048]{3,2,1,0:T(1,128)}, f32[512,2,1,2048]{3,2,1,0:T(1,128)}, f32[512,2,1,2048]{3,2,1,0:T(1,128)}) fusion(f32[512,2,4,2048]{3,2,1,0:T(4,128)} %all-to-all-done.6, s32[]{:T(128)S(6)} %select_n.163, s32[]{:T(128)S(6)} %select_n.166, s32[]{:T(128)S(6)} %select_n.165, ...), kind=kLoop, calls=%fused_computation.29 | loop fusion | bytes 67108880 | tf_op jit(solution)/shard_map/dynamic_slice | solution.py:22
  966.2 2.9 collective-permute-start.2
  970.5 8.0 scatter_custom_fusion.3
  979.8 15.5 scatter_custom_fusion.1
  996.5 702.4 %all-to-all-done.2 = f32[512,2,8,1024]{0,3,1,2:T(8,128)} async-done(((f32[512,2,8,1024]{0,3,1,2:T(8,128)}), f32[512,2,8,1024]{0,3,1,2:T(8,128)}, u32[]{:S(2)}, u32[]{:S(2)}) %all-to-all-start.2) | async-done | bytes 33554464 | tf_op jit(solution)/shard_map/all_to_all | solution.py:121
  1698.9 31.9 %copy.44 = f32[512,2,8,1024]{3,0,1,2:T(8,128)} copy(f32[512,2,8,1024]{0,3,1,2:T(8,128)} %all-to-all-done.2) | data formatting | bytes 67108864 | tf_op jit(solution)/shard_map/all_to_all | solution.py:121
  1730.7 23.4 copy.45
  1754.1 9.7 all-to-all-start.3
  1764.1 9.1 pad_maximum_fusion.2
  1773.3 38.7 %pad_maximum_fusion = f32[4,512,2,1,2048]{4,3,2,1,0:T(1,128)} fusion(f32[1,512,2,1,2048]{4,3,2,1,0:T(1,128)} %bitcast.32, f32[1,512,2,1,2048]{4,3,2,1,0:T(1,128)} %bitcast.31, f32[1,512,2,1,2048]{4,3,2,1,0:T(1,128)} %bitcast.30, f32[1,512,2,1,2048]{4,3,2,1,0:T(1,128)} %get-tuple-element.10), kind=kLoop, calls=%fused_computation.13 | loop fusion | flops 25165824 | bytes 67108864 | tf_op jit(solution)/shard_map/stack | solution.py:26
  1811.9 20.3 fusion.32
  1832.2 8.5 copy.72
  1840.7 7.7 copy.70
  1848.3 13.8 gather_fusion.4
  1862.2 24.9 gather_fusion.3
  1887.1 18.7 copy.71
  1905.8 25.2 gather_fusion.2
  1931.0 22.7 pad_maximum_fusion.1
  1953.7 39.5 %gather_fusion.1 = f32[1024,2,2048]{2,1,0:T(2,128)} fusion(f32[2048,2,2048]{2,1,0:T(2,128)} %bitcast.153, s32[1024]{0:T(1024)S(1)} %copy-done.5), kind=kCustom, calls=%fused_computation.5 | custom fusion | bytes 33558528 | tf_op jit(solution)/shard_map/jit(_take)/gather | solution.py:74
  1993.2 25.0 copy.50
  2018.1 11.5 broadcast_select_fusion.3
  2029.6 96.5 %all-to-all-done.3 = f32[8,4,128,2,1024]{4,2,3,0,1:T(8,128)} async-done(((f32[8,4,128,2,1024]{4,2,3,0,1:T(8,128)}), f32[8,4,128,2,1024]{4,2,3,0,1:T(8,128)}, u32[]{:S(2)}, u32[]{:S(2)}) %all-to-all-start.3) | async-done | bytes 33554464 | tf_op jit(solution)/shard_map/all_to_all | solution.py:127
  2126.1 23.4 copy.46
  2149.4 55.0 %copy.47 = f32[4096,2,1024]{2,1,0:T(2,128)} copy(f32[4096,2,1024]{2,0,1:T(8,128)} %bitcast.148) | data formatting | bytes 67108864 | tf_op jit(solution)/shard_map/reshape | solution.py:131
  2204.5 54.2 %gather_fusion = f32[2048,2,1024]{2,1,0:T(2,128)} fusion(f32[4096,2,1024]{2,1,0:T(2,128)} %copy.47, s32[2048]{0:T(1024)S(1)} %copy-done.2), kind=kCustom, calls=%fused_computation.4 | custom fusion | bytes 33562624 | tf_op jit(solution)/shard_map/jit(_take)/gather | solution.py:74
  2258.7 14.0 broadcast_select_fusion.2
  2272.7 19.8 fusion.33
  2293.1 17.7 fusion.1
  2310.8 16.9 fusion.2
  2327.8 13.5 fusion.3
  2341.3 13.8 add_bitcast_fusion.1
  2355.1 13.5 subtract_bitcast_fusion.1
  2368.7 2.4 pad_maximum_fusion.4
  2371.3 51.0 %reduce-scatter.3.cloned.1.call-done = f32[256,2,512]{2,0,1:T(8,128)} async-done(((f32[1024,2,512]{2,0,1:T(8,128)}), f32[256,2,512]{2,0,1:T(8,128)}) %reduce-scatter.3.cloned.1.call-update) | async-done | bytes 1048592 | tf_op jit(solution)/shard_map/reduce_scatter | solution.py:149
  2422.3 2.3 broadcast_multiply_fusion
  2424.7 52.7 %all-gather.5.cloned.1.call-done = f32[1024,2,512]{2,0,1:T(8,128)} async-done(((f32[256,2,512]{2,0,1:T(8,128)}), f32[1024,2,512]{2,0,1:T(8,128)}) %all-gather.5.cloned.1.call-update) | async-done | bytes 4194320 | tf_op jit(solution)/shard_map/all_gather | solution.py:153
  2477.4 16.4 fusion.7
  2493.9 16.2 fusion.6
  2510.1 15.1 subtract_bitcast_fusion
  2525.2 15.1 add_bitcast_fusion
  2540.3 4.2 pad_maximum_fusion.3
  2544.6 89.7 %reduce-scatter.5.cloned.1.call-done = f32[256,2,512]{2,0,1:T(8,128)} async-done(((f32[2048,2,512]{2,0,1:T(8,128)}), f32[256,2,512]{2,0,1:T(8,128)}) %reduce-scatter.5.cloned.1.call-update) | async-done | bytes 1048592 | tf_op jit(solution)/shard_map/reduce_scatter | solution.py:158
  (99 shorter events, 12.6 us)
Async XLA Ops:
  22.1 12.5 all-to-all-start.4
  35.2 10.7 all-to-all-start
  45.9 50.9 %all-to-all-start.5 = ((s32[512,1,4]{0,1,2:T(1,128)}), s32[512,1,4]{0,1,2:T(1,128)S(1)}, u32[]{:S(2)}, u32[]{:S(2)}) async-start(s32[512,1,4]{0,1,2:T(1,128)} %copy.49), calls=%async_computation.5 | async-start | bytes 16384 | tf_op jit(solution)/shard_map/all_to_all | solution.py:103
  96.7 0.6 copy-start.3
  97.3 73.3 %all-to-all-start.1 = ((s32[8,4,128]{2,0,1:T(8,128)}), s32[8,4,128]{2,0,1:T(8,128)S(1)}, u32[]{:S(2)}, u32[]{:S(2)}) async-start(s32[8,4,128]{2,0,1:T(8,128)} %bitcast.141), calls=%async_computation.1 | async-start | bytes 32768 | tf_op jit(solution)/shard_map/all_to_all | solution.py:128
  170.6 730.5 %all-to-all-start.6 = ((f32[512,2,4,2048]{3,2,1,0:T(4,128)}), f32[512,2,4,2048]{3,2,1,0:T(4,128)}, u32[]{:S(2)}, u32[]{:S(2)}) async-start(f32[512,2,4,2048]{3,2,1,0:T(4,128)} %reshape.232), calls=%async_computation.6 | async-start | bytes 67108864 | tf_op jit(solution)/shard_map/all_to_all | solution.py:101
  901.1 797.8 %all-to-all-start.2 = ((f32[512,2,8,1024]{0,3,1,2:T(8,128)}), f32[512,2,8,1024]{0,3,1,2:T(8,128)}, u32[]{:S(2)}, u32[]{:S(2)}) async-start(f32[512,2,8,1024]{0,3,1,2:T(8,128)} %copy.43), calls=%async_computation.2 | async-start | bytes 67108864 | tf_op jit(solution)/shard_map/all_to_all | solution.py:121
  908.3 1402.5 %all-gather.3.cloned.1.call-start = ((), (), s32[]{:S(2)}) async-start(), calls=%async_computation.9 | async-start | bytes 9437184 | tf_op jit(solution)/shard_map/all_gather | solution.py:144
  908.4 61.4 %copy-start.9 = (s32[8,16]{1,0:T(8,128)S(1)}, s32[8,16]{1,0:T(8,128)}, u32[]{:S(2)}) copy-start(s32[8,16]{1,0:T(8,128)} %param.14) | copy-start | bytes 1540
  908.4 62.1 %copy-start.4 = (s32[512,1,4]{0,1,2:T(1,128)S(1)}, s32[512,1,4]{0,1,2:T(1,128)}, u32[]{:S(2)}) copy-start(s32[512,1,4]{0,1,2:T(1,128)} %copy-done.3) | copy-start | bytes 24580
  966.2 797.9 %collective-permute-start.2 = (f32[512,2,1,2048]{3,2,1,0:T(1,128)}, f32[512,2,1,2048]{3,2,1,0:T(1,128)}, u32[]{:S(2)}, u32[]{:S(2)}) collective-permute-start(f32[512,2,1,2048]{3,2,1,0:T(1,128)} %get-tuple-element.11), channel_id=1, source_target_pairs={{0,3},{1,2},{2,1},{3,0},{4,7},{5,6},{6,5},{7,4},{8,11},{9,10},{10,... | collective-permute-start | bytes 25165832 | tf_op jit(solution)/shard_map/ppermute | solution.py:25
  969.1 795.0 %collective-permute-start.1 = (f32[512,2,1,2048]{3,2,1,0:T(1,128)}, f32[512,2,1,2048]{3,2,1,0:T(1,128)}, u32[]{:S(2)}, u32[]{:S(2)}) collective-permute-start(f32[512,2,1,2048]{3,2,1,0:T(1,128)} %get-tuple-element.12), channel_id=1, source_target_pairs={{0,2},{1,3},{2,0},{3,1},{4,6},{5,7},{6,4},{7,5},{8,10},{9,11},{10,... | collective-permute-start | bytes 25165832 | tf_op jit(solution)/shard_map/ppermute | solution.py:25
  969.7 794.4 %collective-permute-start = (f32[512,2,1,2048]{3,2,1,0:T(1,128)}, f32[512,2,1,2048]{3,2,1,0:T(1,128)}, u32[]{:S(2)}, u32[]{:S(2)}) collective-permute-start(f32[512,2,1,2048]{3,2,1,0:T(1,128)} %get-tuple-element.13), channel_id=1, source_target_pairs={{0,1},{1,0},{2,3},{3,2},{4,5},{5,4},{6,7},{7,6},{8,9},{9,8},{10,11... | collective-permute-start | bytes 25165832 | tf_op jit(solution)/shard_map/ppermute | solution.py:25
  1754.1 372.0 %all-to-all-start.3 = ((f32[8,4,128,2,1024]{4,2,3,0,1:T(8,128)}), f32[8,4,128,2,1024]{4,2,3,0,1:T(8,128)}, u32[]{:S(2)}, u32[]{:S(2)}) async-start(f32[8,4,128,2,1024]{4,2,3,0,1:T(8,128)} %copy.45), calls=%async_computation.3 | async-start | bytes 67108864 | tf_op jit(solution)/shard_map/all_to_all | solution.py:127
  1763.8 658.5 %reduce-scatter.3.cloned.1.call-start = ((), (), s32[]{:S(2)}) async-start(), calls=%async_computation.10 | async-start | bytes 5242880 | tf_op jit(solution)/shard_map/reduce_scatter | solution.py:149
  1931.0 22.7 copy-start.5
  1993.2 25.0 copy-start.8
  2149.4 55.0 %copy-start.2 = (s32[2048]{0:T(1024)S(1)}, s32[2048]{0:T(1024)}, u32[]{:S(2)}) copy-start(s32[2048]{0:T(1024)} %fusion.19) | copy-start | bytes 24580
  2204.5 54.2 %copy-start.6 = (pred[2048]{0:T(1024)(128)(4,1)S(1)}, pred[2048]{0:T(1024)(128)(4,1)}, u32[]{:S(2)}) copy-start(pred[2048]{0:T(1024)(128)(4,1)} %compare_and_fusion) | copy-start | bytes 6148
  2272.7 19.8 copy-start.7
  2310.8 16.9 copy-start
  2310.8 16.9 copy-start.12
  2327.8 27.3 %slice-start = ((s8[8388608]{0:T(1024)(128)(4,1)}), s8[4194304]{0:T(1024)(128)(4,1)S(1)}, s32[]{:S(2)}) async-start(s8[8388608]{0:T(1024)(128)(4,1)} %bitcast.149), calls=%async_computation.13 | async-start | bytes 8388608
  2341.3 13.8 slice-start.1
  2368.7 2.5 copy-start.10
  2368.7 2.5 copy-start.11
  2371.1 106.3 %all-gather.5.cloned.1.call-start = ((), (), s32[]{:S(2)}) async-start(), calls=%async_computation.11 | async-start | bytes 5242880 | tf_op jit(solution)/shard_map/all_gather | solution.py:153
  2424.7 209.6 %reduce-scatter.5.cloned.1.call-start = ((), (), s32[]{:S(2)}) async-start(), calls=%async_computation.12 | async-start | bytes 9437184 | tf_op jit(solution)/shard_map/reduce_scatter | solution.py:158
  2477.4 16.4 copy-start.1
  2477.4 32.7 %slice-start.2 = ((s8[8388608]{0:T(1024)(128)(4,1)}), s8[4194304]{0:T(1024)(128)(4,1)S(1)}, s32[]{:S(2)}) async-start(s8[8388608]{0:T(1024)(128)(4,1)} %bitcast.151), calls=%async_computation.15 | async-start | bytes 8388608
  2493.9 16.2 slice-start.3
Sparse Core Ops, SparseCore 0:
  969.9 175.7 all-gather.2
  2371.3 51.0 reduce-scatter.2
  2424.8 52.5 all-gather.4
  2544.7 89.5 reduce-scatter.4
